TPU v7x, 32 devices: a whole 2x2x4 slice. The times are simulated.
32 devices in a mesh: band: 16 (over z, y, x), lev: 2 (over core).
Axes of the slice: x: 2, y: 2, z: 4, core: 2. Of those that a mesh axis runs over, the one named last changes fastest.
Arguments:
- arrival_adjoint: bfloat16 [160, 64, 1536], P('band', 'lev'), may hold values from -6 to 6
- interp_tiles: bfloat16 [160, 12, 128, 128], P('band'), may hold values from -0.5 to 0.5
- departure_block: int32 [160, 12], P('band'), may hold values from 0 to 239
- slot_wavenumber: int32 [768], replicated, may hold values from 0 to 767, each once
- legendre: bfloat16 [768, 160, 768], P('band', None, 'lev'), may hold values from -0.5 to 0.5
Outputs:
- spectral: bfloat16 [768, 64, 2, 768], P('band', None, None, 'lev')
Inputs may be any that keep to these rules, and one draw needn't show every extreme that they name: `departure_block`: an entry d of the tile at latitude l names latitude L + d // 12 - 5 and longitude block d % 12, where L is the first latitude of l's band of 10. `slot_wavenumber`: each wavenumber below 768 stands in exactly one slot.
All inputs are finite; a program needn't handle non-finite values.
Results may differ from a plain program's by a relative error of at most 0.015.
Values may be sent and summed in bfloat16 or wider, within the bound.
No kernel may reach another device: no remote copies, remote signals or barrier semaphores. Data moves between devices by JAX's collectives and lax.ppermute only.
A program may use at most 128 MiB of HBM per device.

v0:
```python
import math
import jax
import jax.numpy as jnp
from jax import lax
from jax.sharding import PartitionSpec as P


def passed_along(block, axis, distance):
    devices = range(lax.axis_size(axis))
    route = [(i - distance, i) for i in devices if i - distance in devices]
    return lax.ppermute(block, axis, route)


def wave_table(slot_wavenumber, lon_count):
    column = lax.iota(jnp.int32, lon_count)[:, None]
    product = column * slot_wavenumber[None, :] % lon_count
    angle = product.astype(jnp.float32) * (2.0 * math.pi / lon_count)
    factor = math.sqrt(2.0 / lon_count)
    return jnp.stack([jnp.cos(angle) * factor, jnp.sin(angle) * factor]).astype(jnp.bfloat16)


def local(arrival_adjoint, interp_tiles, departure_block, slot_wavenumber, legendre):
    lat_count, level_count, lon_count = arrival_adjoint.shape
    block_count = interp_tiles.shape[1]
    tile_width = interp_tiles.shape[2]
    rim_rows = lat_count // 2
    tiles = arrival_adjoint.reshape(lat_count, level_count, block_count, tile_width)
    contrib = jnp.einsum("lvbi,lbik->lbvk", tiles, interp_tiles, preferred_element_type=jnp.float32)
    contrib = contrib.reshape(lat_count * block_count, level_count * tile_width)
    upper = contrib.astype(jnp.bfloat16)
    lower = (contrib - upper.astype(jnp.float32)).astype(jnp.bfloat16)
    extended = (lat_count + 2 * rim_rows) * block_count
    targets = (lax.iota(jnp.int32, extended)[:, None] == departure_block.reshape(1, -1)).astype(
        jnp.bfloat16
    )
    placed = jnp.dot(targets, upper, preferred_element_type=jnp.float32) + jnp.dot(
        targets, lower, preferred_element_type=jnp.float32
    )
    placed = placed.reshape(lat_count + 2 * rim_rows, block_count, level_count, tile_width)
    from_below = passed_along(
        placed[lat_count + rim_rows :].astype(jnp.bfloat16), "band", 1
    ).astype(jnp.float32)
    from_above = passed_along(placed[:rim_rows].astype(jnp.bfloat16), "band", -1).astype(
        jnp.float32
    )
    grid = placed[rim_rows : rim_rows + lat_count] + jnp.concatenate(
        [from_below, from_above], axis=0
    )
    grid = grid.astype(jnp.bfloat16)
    table = wave_table(slot_wavenumber, lon_count).reshape(2, block_count, tile_width, -1)
    fourier = jnp.einsum("lbvt,cbts->scvl", grid, table, preferred_element_type=jnp.float32).astype(
        jnp.bfloat16
    )
    wave_count = fourier.shape[0]
    flat = fourier.reshape(wave_count, -1)
    shared = lax.all_gather(flat[None], "lev", axis=0, tiled=True)
    owned = lax.all_to_all(shared, "band", split_axis=1, concat_axis=2, tiled=True)
    group_count = owned.shape[0]
    slot_count = owned.shape[1]
    band_count = lax.axis_size("band")
    degree_count = legendre.shape[2]
    owned = owned.reshape(group_count, slot_count, band_count, 2, level_count, lat_count)
    tables = legendre.reshape(slot_count, band_count, lat_count, degree_count)
    spectral = jnp.einsum("gsbcvl,sbln->sgvcn", owned, tables, preferred_element_type=jnp.float32)
    spectral = spectral.reshape(slot_count, group_count * level_count, 2, degree_count)
    degree = lax.axis_index("lev") * degree_count + lax.iota(jnp.int32, degree_count)
    owned_waves = lax.dynamic_slice_in_dim(
        slot_wavenumber, lax.axis_index("band") * slot_count, slot_count
    )
    keep = degree[None, :] >= owned_waves[:, None]
    return jnp.where(keep[:, None, None, :], spectral, 0.0).astype(jnp.bfloat16)


def solution(mesh):
    placed = (
        P("band", "lev", None),
        P("band", None, None, None),
        P("band", None),
        P(),
        P("band", None, "lev"),
    )
    return jax.shard_map(
        local, mesh=mesh, in_specs=placed, out_specs=P("band", None, None, "lev"), check_vma=False
    )
```

profile of v0, /device:TPU:12, one launch (start us, length us, event | category | flops | bytes accessed | tf_op | source)
XLA Modules:
  0.0 174.6 jit_solution(13239174042174371197)
XLA Ops:
  6.5 0.9 eq.18
  7.4 0.4 copy-done
  7.8 3.2 %fusion.20 = f32[10,12,32,128]{3,2,1,0:T(8,128)S(1)} fusion(bf16[10,12,128,128]{3,2,1,0:T(8,128)(2,1)} %param.6, bf16[10,32,1536]{2,1,0:T(8,128)(2,1)S(1)} %copy-done), kind=kOutput, calls=%fused_computation.28 | convolution fusion | flops 125829120 | bytes 6881280 | tf_op jit(solution)/shard_map/lvbi,lbik->lbvk/dot_general | solution.py:28
  11.0 1.5 fusion.15
  12.5 1.6 fusion.30
  14.2 0.1 fusion.29
  14.3 0.1 copy.44
  14.4 3.4 %collective-permute-start = (bf16[5,12,32,128]{3,2,1,0:T(8,128)(2,1)S(1)}, bf16[5,12,32,128]{3,2,1,0:T(8,128)(2,1)S(1)}, u32[]{:S(2)}, u32[]{:S(2)}) collective-permute-start(bf16[5,12,32,128]{3,2,1,0:T(8,128)(2,1)S(1)} %bitcast.81), channel_id=1, source_target_pairs={{0,2},{2,4},{4,6},{6,8},{8,10},{10,12},{12,14},{14,16},{16,18},{18... | collective-permute-start | bytes 1474568 | tf_op jit(solution)/shard_map/ppermute | solution.py:11
  17.8 0.1 copy.45
  18.0 3.3 %collective-permute-start.1 = (bf16[5,12,32,128]{3,2,1,0:T(8,128)(2,1)S(1)}, bf16[5,12,32,128]{3,2,1,0:T(8,128)(2,1)S(1)}, u32[]{:S(2)}, u32[]{:S(2)}) collective-permute-start(bf16[5,12,32,128]{3,2,1,0:T(8,128)(2,1)S(1)} %bitcast.82), channel_id=1, source_target_pairs={{2,0},{4,2},{6,4},{8,6},{10,8},{12,10},{14,12},{16,14},{18,16},{20... | collective-permute-start | bytes 1474568 | tf_op jit(solution)/shard_map/ppermute | solution.py:11
  21.4 0.1 slice_bitcast_fusion
  21.5 0.3 copy.43
  21.9 0.2 copy-done.2
  22.0 20.6 %multiply_convert_fusion.1 = (bf16[1,12,128,768]{3,2,1,0:T(8,128)(2,1)S(1)}, bf16[1,12,128,768]{3,2,1,0:T(8,128)(2,1)S(1)}) fusion(s32[768]{0:T(1024)S(1)} %copy-done.2, s32[12,128]{1,0:T(8,128)S(1)} %multiply_add_fusion), kind=kLoop, calls=%fused_computation.13 | loop fusion | flops 15335424 | bytes 4727808 | tf_op jit(solution)/shard_map/convert.3
  42.6 1.7 fusion.16
  44.3 0.6 copy.25
  44.9 0.4 broadcast_in_dim_reshape.3
  45.3 1.3 copy.26
  46.7 11.0 %all-gather.2.cloned.1.call-done = bf16[2,768,640]{2,1,0:T(8,128)(2,1)} async-done(((bf16[1,768,640]{2,1,0:T(8,128)(2,1)}), bf16[2,768,640]{2,1,0:T(8,128)(2,1)}) %all-gather.2.cloned.1.call-update) | async-done | bytes 1966096 | tf_op jit(solution)/shard_map/all_gather | solution.py:56
  57.7 4.8 %copy.27 = bf16[2,768,640]{2,0,1:T(2,128)(2,1)} copy(bf16[2,768,640]{2,1,0:T(8,128)(2,1)} %all-gather.2.cloned.1.call-done) | data formatting | bytes 3932160 | tf_op jit(solution)/shard_map/all_gather | solution.py:56
  62.6 7.0 %all-to-all-start = ((bf16[2,768,640]{2,0,1:T(2,128)(2,1)}), bf16[2,768,640]{2,0,1:T(2,128)(2,1)S(1)}, u32[]{:S(2)}, u32[]{:S(2)}) async-start(bf16[2,768,640]{2,0,1:T(2,128)(2,1)} %copy.27), calls=%async_computation | async-start | bytes 3932160 | tf_op jit(solution)/shard_map/all_to_all | solution.py:57
  69.5 7.4 %copy.30 = bf16[48,160,384]{2,0,1:T(8,128)(2,1)} copy(bf16[48,160,384]{2,1,0:T(8,128)(2,1)} %param.9) | data formatting | bytes 11796480 | tf_op args[4]
  77.0 0.1 dynamic_slice.3
  77.0 0.1 broadcast_compare_fusion
  77.1 38.1 %all-to-all-done = bf16[2,768,640]{2,0,1:T(2,128)(2,1)S(1)} async-done(((bf16[2,768,640]{2,0,1:T(2,128)(2,1)}), bf16[2,768,640]{2,0,1:T(2,128)(2,1)S(1)}, u32[]{:S(2)}, u32[]{:S(2)}) %all-to-all-start) | async-done | bytes 1966112 | tf_op jit(solution)/shard_map/all_to_all | solution.py:57
  115.3 1.5 copy.28
  116.8 6.7 %copy.29 = bf16[2,48,16,640]{1,2,3,0:T(8,128)(2,1)} copy(bf16[2,48,16,640]{3,1,2,0:T(8,128)(2,1)} %bitcast.75) | data formatting | bytes 3932160 | tf_op jit(solution)/shard_map/all_to_all | solution.py:57
  123.5 15.3 %copy.31 = bf16[2,48,16,2,32,10]{4,2,5,3,0,1:T(8,128)(2,1)} copy(bf16[2,48,16,2,32,10]{1,2,5,4,3,0:T(8,128)(2,1)} %bitcast.72) | data formatting | bytes 3932160 | tf_op jit(solution)/shard_map/reshape | solution.py:62
  138.9 12.0 %fusion.11 = bf16[48,2,32,2,384]{4,2,3,1,0:T(8,128)(2,1)} fusion(bf16[2,48,16,2,32,10]{4,2,5,3,0,1:T(8,128)(2,1)} %copy.31, bf16[48,16,10,384,1,1]{3,0,2,1,5,4:T(8,128)(2,1)} %bitcast.71), kind=kOutput, calls=%fused_computation.18 | convolution fusion | flops 754974720 | bytes 12582912 | tf_op jit(solution)/shard_map/gsbcvl,sbln->sgvcn/dot_general | solution.py:64
  150.9 3.2 %copy.33 = bf16[48,2,32,2,384]{4,2,1,3,0:T(8,128)(2,1)S(1)} copy(bf16[48,2,32,2,384]{4,2,3,1,0:T(8,128)(2,1)} %fusion.11) | data formatting | bytes 9437184 | tf_op jit(solution)/shard_map/gsbcvl,sbln->sgvcn/transpose | solution.py:64
  154.1 4.2 %fusion = bf16[48,64,2,384]{3,1,2,0:T(8,128)(2,1)} fusion(bf16[48,2,32,2,384]{4,2,1,3,0:T(8,128)(2,1)S(1)} %copy.33, pred[48,384]{1,0:T(8,128)(4,1)S(1)} %broadcast_compare_fusion), kind=kLoop, calls=%fused_computation.1 | loop fusion | flops 2359296 | bytes 9455616 | tf_op jit(solution)/shard_map/convert_element_type | solution.py:71
  158.4 9.4 %copy.34 = bf16[48,64,2,384]{3,2,1,0:T(2,128)(2,1)} copy(bf16[48,64,2,384]{3,1,2,0:T(8,128)(2,1)} %fusion) | data formatting | bytes 9437184 | tf_op jit(solution)/shard_map/convert_element_type | solution.py:71
  (12 shorter events, 0.1 us)
Async XLA Ops:
  6.5 1.2 copy-start
  6.5 51.2 %all-gather.2.cloned.1.call-start = ((), (), s32[]{:S(2)}) async-start(), calls=%async_computation.1 | async-start | bytes 2949120 | tf_op jit(solution)/shard_map/all_gather | solution.py:56
  14.4 28.2 %collective-permute-start = (bf16[5,12,32,128]{3,2,1,0:T(8,128)(2,1)S(1)}, bf16[5,12,32,128]{3,2,1,0:T(8,128)(2,1)S(1)}, u32[]{:S(2)}, u32[]{:S(2)}) collective-permute-start(bf16[5,12,32,128]{3,2,1,0:T(8,128)(2,1)S(1)} %bitcast.81), channel_id=1, source_target_pairs={{0,2},{2,4},{4,6},{6,8},{8,10},{10,12},{12,14},{14,16},{16,18},{18... | collective-permute-start | bytes 1474568 | tf_op jit(solution)/shard_map/ppermute | solution.py:11
  18.0 24.7 %collective-permute-start.1 = (bf16[5,12,32,128]{3,2,1,0:T(8,128)(2,1)S(1)}, bf16[5,12,32,128]{3,2,1,0:T(8,128)(2,1)S(1)}, u32[]{:S(2)}, u32[]{:S(2)}) collective-permute-start(bf16[5,12,32,128]{3,2,1,0:T(8,128)(2,1)S(1)} %bitcast.82), channel_id=1, source_target_pairs={{2,0},{4,2},{6,4},{8,6},{10,8},{12,10},{14,12},{16,14},{18,16},{20... | collective-permute-start | bytes 1474568 | tf_op jit(solution)/shard_map/ppermute | solution.py:11
  21.3 0.7 copy-start.2
  62.6 52.7 %all-to-all-start = ((bf16[2,768,640]{2,0,1:T(2,128)(2,1)}), bf16[2,768,640]{2,0,1:T(2,128)(2,1)S(1)}, u32[]{:S(2)}, u32[]{:S(2)}) async-start(bf16[2,768,640]{2,0,1:T(2,128)(2,1)} %copy.27), calls=%async_computation | async-start | bytes 3932160 | tf_op jit(solution)/shard_map/all_to_all | solution.py:57
  154.1 13.6 %copy-start.1 = (bf16[10,32,1536]{2,1,0:T(8,128)(2,1)S(1)}, bf16[10,32,1536]{2,1,0:T(8,128)(2,1)}, u32[]{:S(2)}) copy-start(bf16[10,32,1536]{2,1,0:T(8,128)(2,1)} %param.5) | copy-start | bytes 2949124
Sparse Core Ops, SparseCore 0:
  46.8 10.8 all-gather.1
where the time goes:
time: 175 us
  local copies, waits for them, and re-layouts  53.1 us (30%)
  waiting for transfers between devices  49.2 us (28%)
  other arithmetic  24.9 us (14%)
  matrix products  20.1 us (11%)
  starting transfers between devices  13.7 us (8%)
  between operations  13.6 us (8%)
    all_to_all x1, waiting for transfers between devices, local(): lax.all_to_all(shared, 'band', split_axis=1, concat_axis=2, tiled=True)  38.1 us
    another operation x1, other arithmetic  20.6 us
    reshape x1, local copies, waits for them, and re-layouts, local(): owned.reshape(group_count, slot_count, band_count, 2, level_count, lat_co...  15.3 us
    dot_general x1, matrix products, local(): jnp.einsum('gsbcvl,sbln->sgvcn', owned, tables, preferred_element_type=jn...  12 us
    all_gather x1, waiting for transfers between devices, local(): shared = lax.all_gather(flat[None], 'lev', axis=0, tiled=True)  11 us
    convert_element_type x1, local copies, waits for them, and re-layouts, local(): return jnp.where(keep[:, None, None, :], spectral, 0.0).astype(jnp.bfloat16)  9.37 us
    unnamed x13, local copies, waits for them, and re-layouts  8.71 us
    all_to_all x2, local copies, waits for them, and re-layouts, local(): lax.all_to_all(shared, 'band', split_axis=1, concat_axis=2, tiled=True)  8.26 us
  transfers between devices with their start and end apart: 4, of which 2 were waited for; matrix products, arithmetic and copies ran while one was open for 16% of the time, Pallas kernels for 0%

commit v1 on v0

--- a/solution.py
+++ b/solution.py
@@ -3,6 +3,13 @@
 import jax.numpy as jnp
 from jax import lax
 from jax.sharding import PartitionSpec as P
+
+
+def trade_parts(x, mesh_axis, split, join):
+    peers = lax.axis_size(mesh_axis)
+    blocks = jnp.stack(jnp.split(x, peers, axis=split), axis=0)
+    blocks = lax.all_to_all(blocks, mesh_axis, split_axis=0, concat_axis=0)
+    return jnp.concatenate(blocks, axis=join)
 
 
 def passed_along(block, axis, distance):
@@ -54,7 +61,7 @@
     wave_count = fourier.shape[0]
     flat = fourier.reshape(wave_count, -1)
     shared = lax.all_gather(flat[None], "lev", axis=0, tiled=True)
-    owned = lax.all_to_all(shared, "band", split_axis=1, concat_axis=2, tiled=True)
+    owned = trade_parts(shared, "band", 1, 2)
     group_count = owned.shape[0]
     slot_count = owned.shape[1]
     band_count = lax.axis_size("band")

time: 175 us -> 193 us (1.10)
  local copies, waits for them, and re-layouts: 53.1 us -> 70.4 us
    unnamed x13 -> x28, local copies, waits for them, and re-layouts: 8.71 us -> 32.3 us
    another operation x0 -> x2, local copies, waits for them, and re-layouts: none -> 16.9 us  [the longest x1 15.3 us: local(): owned.reshape(group_count, slot_count, band_count, 2, level_count, lat_co...]
    reshape x1 -> x0, local copies, waits for them, and re-layouts: 15.3 us -> none  [local(): owned.reshape(group_count, slot_count, band_count, 2, level_count, lat_co...]
    all_gather x1 -> x0, local copies, waits for them, and re-layouts: 4.84 us -> none  [local(): shared = lax.all_gather(flat[None], 'lev', axis=0, tiled=True)]
    all_to_all x2 -> x1, local copies, waits for them, and re-layouts: 8.26 us -> 5.27 us  [trade_parts(): blocks = lax.all_to_all(blocks, mesh_axis, split_axis=0, concat_axis=0)]
  transfers between devices with their start and end apart: 4 -> 4, of which waited for: 2 -> 2; matrix products, arithmetic and copies ran while one was open for 16% -> 15% of each run, Pallas kernels for 0% -> 0%
where the time goes in v1:
time: 193 us; the launch traced here: 192 us
  local copies, waits for them, and re-layouts  70.4 us (36%)
  waiting for transfers between devices  49.2 us (25%)
  other arithmetic  24.9 us (13%)
  matrix products  20.1 us (10%)
  starting transfers between devices  13.7 us (7%)
  between operations  13.6 us (7%)
    all_to_all x1, waiting for transfers between devices, trade_parts(): blocks = lax.all_to_all(blocks, mesh_axis, split_axis=0, concat_axis=0)  38.1 us
    unnamed x28, local copies, waits for them, and re-layouts  32.3 us
    another operation x1, other arithmetic  20.6 us
    another operation x1, local copies, waits for them, and re-layouts, local(): owned.reshape(group_count, slot_count, band_count, 2, level_count, lat_co...  15.3 us
    dot_general x1, matrix products, local(): jnp.einsum('gsbcvl,sbln->sgvcn', owned, tables, preferred_element_type=jn...  12 us
    all_gather x1, waiting for transfers between devices, local(): shared = lax.all_gather(flat[None], 'lev', axis=0, tiled=True)  11 us
    convert_element_type x1, local copies, waits for them, and re-layouts, local(): return jnp.where(keep[:, None, None, :], spectral, 0.0).astype(jnp.bfloat16)  9.46 us
    all_to_all x1, starting transfers between devices, trade_parts(): blocks = lax.all_to_all(blocks, mesh_axis, split_axis=0, concat_axis=0)  6.96 us
  transfers between devices with their start and end apart: 4, of which 2 were waited for; matrix products, arithmetic and copies ran while one was open for 15% of the time, Pallas kernels for 0%

profile of v1, /device:TPU:12, one launch (start us, length us, event | category | flops | bytes accessed | tf_op | source)
XLA Modules:
  0.0 192.0 jit_solution(2978415815893470104)
XLA Ops:
  7.8 3.2 %fusion.20 = f32[10,12,32,128]{3,2,1,0:T(8,128)S(1)} fusion(bf16[10,12,128,128]{3,2,1,0:T(8,128)(2,1)} %param.6, bf16[10,32,1536]{2,1,0:T(8,128)(2,1)S(1)} %copy-done), kind=kOutput, calls=%fused_computation.28 | convolution fusion | flops 125829120 | bytes 6881280 | tf_op jit(solution)/shard_map/lvbi,lbik->lbvk/dot_general | solution.py:35
  12.5 1.6 fusion.46
  14.4 3.4 %collective-permute-start = (bf16[5,12,32,128]{3,2,1,0:T(8,128)(2,1)S(1)}, bf16[5,12,32,128]{3,2,1,0:T(8,128)(2,1)S(1)}, u32[]{:S(2)}, u32[]{:S(2)}) collective-permute-start(bf16[5,12,32,128]{3,2,1,0:T(8,128)(2,1)S(1)} %bitcast.143), channel_id=1, source_target_pairs={{0,2},{2,4},{4,6},{6,8},{8,10},{10,12},{12,14},{14,16},{16,18},{18... | collective-permute-start | bytes 1474568 | tf_op jit(solution)/shard_map/ppermute | solution.py:18
  18.0 3.3 %collective-permute-start.1 = (bf16[5,12,32,128]{3,2,1,0:T(8,128)(2,1)S(1)}, bf16[5,12,32,128]{3,2,1,0:T(8,128)(2,1)S(1)}, u32[]{:S(2)}, u32[]{:S(2)}) collective-permute-start(bf16[5,12,32,128]{3,2,1,0:T(8,128)(2,1)S(1)} %bitcast.144), channel_id=1, source_target_pairs={{2,0},{4,2},{6,4},{8,6},{10,8},{12,10},{14,12},{16,14},{18,16},{20... | collective-permute-start | bytes 1474568 | tf_op jit(solution)/shard_map/ppermute | solution.py:18
  22.2 20.6 %multiply_convert_fusion.1 = (bf16[1,12,128,768]{3,2,1,0:T(8,128)(2,1)S(1)}, bf16[1,12,128,768]{3,2,1,0:T(8,128)(2,1)S(1)}) fusion(s32[768]{0:T(1024)S(1)} %copy-done.2, s32[12,128]{1,0:T(8,128)S(1)} %multiply_add_fusion), kind=kLoop, calls=%fused_computation.13 | loop fusion | flops 15335424 | bytes 4727808 | tf_op jit(solution)/shard_map/convert.3
  42.8 1.7 fusion.16
  46.8 11.0 %all-gather.2.cloned.1.call-done = bf16[2,768,640]{2,1,0:T(8,128)(2,1)} async-done(((bf16[1,768,640]{2,1,0:T(8,128)(2,1)}), bf16[2,768,640]{2,1,0:T(8,128)(2,1)}) %all-gather.2.cloned.1.call-update) | async-done | bytes 1966096 | tf_op jit(solution)/shard_map/all_gather | solution.py:63
  57.9 1.6 fusion.41
  59.4 1.6 fusion.40
  61.0 1.6 fusion.39
  62.6 1.6 fusion.38
  64.1 1.6 fusion.37
  65.7 1.6 fusion.36
  67.2 1.6 fusion.35
  68.8 1.6 fusion.34
  70.4 1.6 fusion.33
  71.9 1.6 fusion.32
  73.5 1.6 fusion.31
  75.0 1.6 fusion.30
  76.6 1.6 fusion.29
  78.2 1.6 fusion.28
  79.7 1.6 fusion.27
  81.3 1.6 fusion.26
  82.8 7.0 %all-to-all-start = ((bf16[16,2,48,640]{3,2,1,0:T(8,128)(2,1)}), bf16[16,2,48,640]{3,2,1,0:T(8,128)(2,1)S(1)}, u32[]{:S(2)}, u32[]{:S(2)}) async-start(bf16[16,2,48,640]{3,2,1,0:T(8,128)(2,1)} %fusion.26), calls=%async_computation | async-start | bytes 3932160 | tf_op jit(solution)/shard_map/all_to_all | solution.py:11
  89.8 7.4 %copy.20 = bf16[48,160,384]{2,0,1:T(8,128)(2,1)} copy(bf16[48,160,384]{2,1,0:T(8,128)(2,1)} %param.9) | data formatting | bytes 11796480 | tf_op args[4]
  97.4 38.1 %all-to-all-done = bf16[16,2,48,640]{3,2,1,0:T(8,128)(2,1)S(1)} async-done(((bf16[16,2,48,640]{3,2,1,0:T(8,128)(2,1)}), bf16[16,2,48,640]{3,2,1,0:T(8,128)(2,1)S(1)}, u32[]{:S(2)}, u32[]{:S(2)}) %all-to-all-start) | async-done | bytes 1966112 | tf_op jit(solution)/shard_map/all_to_all | solution.py:11
  135.5 5.3 %copy.19 = bf16[16,2,48,640]{2,0,3,1:T(8,128)(2,1)} copy(bf16[16,2,48,640]{3,2,1,0:T(8,128)(2,1)S(1)} %all-to-all-done) | data formatting | bytes 3932160 | tf_op jit(solution)/shard_map/all_to_all | solution.py:11
  140.8 15.3 %copy.21 = bf16[2,48,16,2,32,10]{4,2,5,3,0,1:T(8,128)(2,1)} copy(bf16[2,48,16,2,32,10]{1,2,5,4,3,0:T(8,128)(2,1)} %bitcast.135) | data formatting | bytes 3932160 | tf_op jit(solution)/shard_map/reshape;reshape | solution.py:69
  156.2 12.0 %fusion.11 = bf16[48,2,32,2,384]{4,2,3,1,0:T(8,128)(2,1)} fusion(bf16[2,48,16,2,32,10]{4,2,5,3,0,1:T(8,128)(2,1)} %copy.21, bf16[48,16,10,384,1,1]{3,0,2,1,5,4:T(8,128)(2,1)} %bitcast.134), kind=kOutput, calls=%fused_computation.18 | convolution fusion | flops 754974720 | bytes 12582912 | tf_op jit(solution)/shard_map/gsbcvl,sbln->sgvcn/dot_general | solution.py:71
  168.2 3.2 %copy.23 = bf16[48,2,32,2,384]{4,2,1,3,0:T(8,128)(2,1)S(1)} copy(bf16[48,2,32,2,384]{4,2,3,1,0:T(8,128)(2,1)} %fusion.11) | data formatting | bytes 9437184 | tf_op jit(solution)/shard_map/gsbcvl,sbln->sgvcn/transpose | solution.py:71
  171.4 4.2 %fusion = bf16[48,64,2,384]{3,1,2,0:T(8,128)(2,1)} fusion(bf16[48,2,32,2,384]{4,2,1,3,0:T(8,128)(2,1)S(1)} %copy.23, pred[48,384]{1,0:T(8,128)(4,1)S(1)} %broadcast_compare_fusion), kind=kLoop, calls=%fused_computation.1 | loop fusion | flops 2359296 | bytes 9455616 | tf_op jit(solution)/shard_map/convert_element_type | solution.py:78
  175.7 9.5 %copy.24 = bf16[48,64,2,384]{3,2,1,0:T(2,128)(2,1)} copy(bf16[48,64,2,384]{3,1,2,0:T(8,128)(2,1)} %fusion) | data formatting | bytes 9437184 | tf_op jit(solution)/shard_map/convert_element_type | solution.py:78
  (26 shorter events, 6.4 us)
Async XLA Ops:
  6.5 1.2 copy-start
  6.5 51.3 %all-gather.2.cloned.1.call-start = ((), (), s32[]{:S(2)}) async-start(), calls=%async_computation.1 | async-start | bytes 2949120 | tf_op jit(solution)/shard_map/all_gather | solution.py:63
  14.4 28.3 %collective-permute-start = (bf16[5,12,32,128]{3,2,1,0:T(8,128)(2,1)S(1)}, bf16[5,12,32,128]{3,2,1,0:T(8,128)(2,1)S(1)}, u32[]{:S(2)}, u32[]{:S(2)}) collective-permute-start(bf16[5,12,32,128]{3,2,1,0:T(8,128)(2,1)S(1)} %bitcast.143), channel_id=1, source_target_pairs={{0,2},{2,4},{4,6},{6,8},{8,10},{10,12},{12,14},{14,16},{16,18},{18... | collective-permute-start | bytes 1474568 | tf_op jit(solution)/shard_map/ppermute | solution.py:18
  18.0 24.8 %collective-permute-start.1 = (bf16[5,12,32,128]{3,2,1,0:T(8,128)(2,1)S(1)}, bf16[5,12,32,128]{3,2,1,0:T(8,128)(2,1)S(1)}, u32[]{:S(2)}, u32[]{:S(2)}) collective-permute-start(bf16[5,12,32,128]{3,2,1,0:T(8,128)(2,1)S(1)} %bitcast.144), channel_id=1, source_target_pairs={{2,0},{4,2},{6,4},{8,6},{10,8},{12,10},{14,12},{16,14},{18,16},{20... | collective-permute-start | bytes 1474568 | tf_op jit(solution)/shard_map/ppermute | solution.py:18
  21.5 0.7 copy-start.2
  82.8 52.7 %all-to-all-start = ((bf16[16,2,48,640]{3,2,1,0:T(8,128)(2,1)}), bf16[16,2,48,640]{3,2,1,0:T(8,128)(2,1)S(1)}, u32[]{:S(2)}, u32[]{:S(2)}) async-start(bf16[16,2,48,640]{3,2,1,0:T(8,128)(2,1)} %fusion.26), calls=%async_computation | async-start | bytes 3932160 | tf_op jit(solution)/shard_map/all_to_all | solution.py:11
  175.7 9.5 %copy-start.1 = (bf16[10,32,1536]{2,1,0:T(8,128)(2,1)S(1)}, bf16[10,32,1536]{2,1,0:T(8,128)(2,1)}, u32[]{:S(2)}) copy-start(bf16[10,32,1536]{2,1,0:T(8,128)(2,1)} %param.5) | copy-start | bytes 2949124
Sparse Core Ops, SparseCore 0:
  46.9 10.8 all-gather.1
